TPU v7x, 32 devices: a whole 2x2x4 slice. The times are simulated.
32 devices in a mesh: ctx: 16 (over z, y, core), tp: 2 (over x).
Axes of the slice: x: 2, y: 2, z: 4, core: 2. Of those that a mesh axis runs over, the one named last changes fastest.
Arguments:
- tokens: bfloat16 [4096, 1024], P('ctx'), may hold values from -6 to 6
- seq_ids: int32 [4096], P('ctx'), may hold values from 0 to 3, never falling along the last dimension, each value on 1 to 2048 neighbouring positions
- attention_norm_gain: float32 [1024], replicated, may hold values from 0.5 to 1.5
- qkv_weight: bfloat16 [1024, 3, 1024], P(None, None, 'tp'), may hold values from -1 to 1, as said below
- out_weight: bfloat16 [1024, 1024], P('tp'), may hold values from -1.5 to 1.5
- feedforward_norm_gain: float32 [1024], replicated, may hold values from 0.5 to 1.5
- mlp_in_weight: bfloat16 [1024, 2, 2624], P(None, None, 'tp'), may hold values from -0.1875 to 0.1875
- mlp_out_weight: bfloat16 [2624, 1024], P('tp'), may hold values from -0.125 to 0.125
- grad_out: bfloat16 [4096, 1024], P('ctx'), may hold values from -6 to 6
Outputs:
- output: bfloat16 [4096, 1024], P('ctx')
- grad_tokens: float32 [4096, 1024], P('ctx')
- grad_norm1_gain: float32 [1024], replicated
- grad_qkv_weight: float32 [1024, 3, 1024], P(None, None, 'tp')
- grad_out_weight: float32 [1024, 1024], P('tp')
- grad_norm2_gain: float32 [1024], replicated
- grad_mlp_in_weight: float32 [1024, 2, 2624], P(None, None, 'tp')
- grad_mlp_out_weight: float32 [2624, 1024], P('tp')
Inputs may be any that keep to these rules, and one draw needn't show every extreme that they name: `seq_ids`: never falling along the tokens; every one of the 4 sequences has at least one token and one has exactly 2048. `qkv_weight`: A projection matrix with entries of order 1024^(-1/2).
All inputs are finite; a program needn't handle non-finite values.
Results may differ from a plain program's by a relative error of at most 0.025.
Values may be sent and summed in bfloat16 or wider, within the bound.
No kernel may reach another device: no remote copies, remote signals or barrier semaphores. Data moves between devices by JAX's collectives and lax.ppermute only.
A program may use at most 256 MiB of HBM per device.

v0:
```python
import math
import jax
import jax.numpy as jnp
from jax import lax
from jax.sharding import PartitionSpec as P

HD = 64
EPS = 1e-05
BASE = 160000.0
MASKED = -1e30
ROOT_HALF = 0.7071067811865476
INV_ROOT_TWO_PI = 0.3989422804014327


def layer_normalize(values_in, norm_gain_vector):
    token_average = jnp.mean(values_in, axis=-1, keepdims=True)
    centered_input = values_in - token_average
    inverse_deviation = lax.rsqrt(
        jnp.mean(centered_input * centered_input, axis=-1, keepdims=True) + EPS
    )
    standardized_input = centered_input * inverse_deviation
    return (standardized_input, inverse_deviation, standardized_input * norm_gain_vector)


def layer_normalize_backward(
    output_gradient, standardized_input, inverse_deviation, norm_gain_vector
):
    normalized_gradient = output_gradient * norm_gain_vector
    correction_term = jnp.mean(
        normalized_gradient, axis=-1, keepdims=True
    ) + standardized_input * jnp.mean(
        normalized_gradient * standardized_input, axis=-1, keepdims=True
    )
    return (
        inverse_deviation * (normalized_gradient - correction_term),
        jnp.sum(output_gradient * standardized_input, axis=0),
    )


def gelu_value(v):
    return v * 0.5 * (1.0 + lax.erf(v * ROOT_HALF))


def gelu_slope(v):
    return 0.5 * (1.0 + lax.erf(v * ROOT_HALF)) + v * jnp.exp(-0.5 * v * v) * INV_ROOT_TWO_PI


def rope_tables(positions, head_size):
    half = head_size // 2
    inverse = BASE ** (-(jnp.arange(half, dtype=jnp.float32) * (2.0 / head_size)))
    angle = positions.astype(jnp.float32)[:, None] * inverse[None, :]
    angle = jnp.concatenate([angle, angle], axis=-1)
    return (jnp.cos(angle), jnp.sin(angle))


def rotate(field, cosine, sine):
    half = field.shape[-1] // 2
    turned = jnp.concatenate([-field[..., half:], field[..., :half]], axis=-1)
    return field * cosine[:, None, :] + turned * sine[:, None, :]


def unrotate(grad, cosine, sine):
    half = grad.shape[-1] // 2
    lifted = grad * sine[:, None, :]
    back = jnp.concatenate([lifted[..., half:], -lifted[..., :half]], axis=-1)
    return grad * cosine[:, None, :] + back


def block_grads(q_rows, do_rows, lse_rows, delta_rows, seq_rows, k_rows, v_rows, seq_cols, scale):
    f32 = jnp.float32
    scores = jnp.einsum("qhd,khd->hqk", q_rows, k_rows, preferred_element_type=f32) * scale
    same = (seq_rows[:, None] == seq_cols[None, :])[None]
    probs = jnp.where(same, jnp.exp(scores - lse_rows.T[:, :, None]), 0.0)
    grad_v = jnp.einsum(
        "hqk,qhd->khd", probs.astype(jnp.bfloat16), do_rows, preferred_element_type=f32
    )
    grad_p = jnp.einsum("qhd,khd->hqk", do_rows, v_rows, preferred_element_type=f32)
    grad_s = (probs * (grad_p - delta_rows.T[:, :, None])).astype(jnp.bfloat16)
    grad_q = jnp.einsum("hqk,khd->qhd", grad_s, k_rows, preferred_element_type=f32) * scale
    grad_k = jnp.einsum("hqk,qhd->khd", grad_s, q_rows, preferred_element_type=f32) * scale
    return (grad_q, grad_k, grad_v)


def per_device(
    tokens,
    seq_ids,
    attention_norm_gain,
    qkv_weight,
    out_weight,
    feedforward_norm_gain,
    mlp_in_weight,
    mlp_out_weight,
    grad_out,
):
    f32 = jnp.float32
    bf16 = jnp.bfloat16
    tok_rows, width = tokens.shape
    local_cols = qkv_weight.shape[2]
    heads_here = local_cols // HD
    hidden_here = mlp_in_weight.shape[2]
    scale = 1.0 / math.sqrt(HD)
    input_tokens = tokens.astype(f32)
    attention_standardized, attention_inverse_deviation, attention_normed_input = layer_normalize(
        input_tokens, attention_norm_gain
    )
    first = attention_normed_input.astype(bf16)
    qkv_flat = qkv_weight.reshape(width, 3 * local_cols)
    proj = jnp.dot(first, qkv_flat, preferred_element_type=f32).reshape(tok_rows, 3, heads_here, HD)
    positions = lax.axis_index("ctx") * tok_rows + jnp.arange(tok_rows, dtype=jnp.int32)
    cosine, sine = rope_tables(positions, HD)
    query = rotate(proj[:, 0], cosine, sine).astype(bf16)
    keys = rotate(proj[:, 1], cosine, sine).astype(bf16)
    values = proj[:, 2].astype(bf16)
    keys_flat = keys.reshape(tok_rows, local_cols)
    values_flat = values.reshape(tok_rows, local_cols)
    run_max = jnp.full((heads_here, tok_rows), MASKED, f32)
    key_piece = lax.all_gather(keys_flat, "ctx", axis=0, tiled=True)
    value_piece = lax.all_gather(values_flat, "ctx", axis=0, tiled=True)
    seq_piece = lax.all_gather(seq_ids, "ctx", axis=0, tiled=True)
    count = key_piece.shape[0]
    key_heads = key_piece.reshape(count, heads_here, HD)
    value_heads = value_piece.reshape(count, heads_here, HD)
    scores = jnp.einsum("qhd,khd->hqk", query, key_heads, preferred_element_type=f32) * scale
    same = (seq_ids[:, None] == seq_piece[None, :])[None]
    top = jnp.max(jnp.where(same, scores, MASKED), axis=-1)
    new_max = jnp.maximum(run_max, top)
    weights = jnp.where(same, jnp.exp(scores - new_max[..., None]), 0.0)
    run_sum = jnp.sum(weights, axis=-1)
    added = jnp.einsum(
        "hqk,khd->hqd", weights.astype(bf16), value_heads, preferred_element_type=f32
    )
    run_acc = added
    run_max, run_sum, run_acc = (new_max, run_sum, run_acc)
    attended = (run_acc / run_sum[..., None]).transpose(1, 0, 2).astype(bf16)
    lse = (run_max + jnp.log(run_sum)).T
    attended_flat = attended.reshape(tok_rows, local_cols)
    attn_part = jnp.dot(attended_flat, out_weight, preferred_element_type=f32)
    residual_middle = input_tokens + lax.psum(attn_part.astype(jnp.bfloat16), "tp").astype(
        jnp.float32
    )
    feedforward_standardized, feedforward_inverse_deviation, feedforward_normed_input = (
        layer_normalize(residual_middle, feedforward_norm_gain)
    )
    second = feedforward_normed_input.astype(bf16)
    in_flat = mlp_in_weight.reshape(width, 2 * hidden_here)
    mixed = jnp.dot(second, in_flat, preferred_element_type=f32).reshape(tok_rows, 2, hidden_here)
    act_in = mixed[:, 0]
    gate = mixed[:, 1]
    hidden = (gelu_value(act_in) * gate).astype(bf16)
    ffn_part = jnp.dot(hidden, mlp_out_weight, preferred_element_type=f32)
    output = (
        residual_middle + lax.psum(ffn_part.astype(jnp.bfloat16), "tp").astype(jnp.float32)
    ).astype(bf16)
    upstream = grad_out.astype(f32)
    grad_w_out = jnp.dot(hidden.T, grad_out, preferred_element_type=f32)
    grad_hidden = jnp.dot(grad_out, mlp_out_weight.T, preferred_element_type=f32)
    grad_mixed = jnp.stack(
        [grad_hidden * gate * gelu_slope(act_in), grad_hidden * gelu_value(act_in)], axis=1
    ).astype(bf16)
    grad_mixed_flat = grad_mixed.reshape(tok_rows, 2 * hidden_here)
    grad_w_in = jnp.dot(second.T, grad_mixed_flat, preferred_element_type=f32).reshape(
        width, 2, hidden_here
    )
    second_part = jnp.dot(grad_mixed_flat, in_flat.T, preferred_element_type=f32)
    feedforward_norm_gradient = lax.psum(second_part.astype(jnp.bfloat16), "tp").astype(jnp.float32)
    feedforward_normed_gradient, feedforward_gain_gradient = layer_normalize_backward(
        feedforward_norm_gradient,
        feedforward_standardized,
        feedforward_inverse_deviation,
        feedforward_norm_gain,
    )
    grad_mid = upstream + feedforward_normed_gradient
    grad_mid_b = grad_mid.astype(bf16)
    grad_w_attn = jnp.dot(attended_flat.T, grad_mid_b, preferred_element_type=f32)
    grad_att = (
        jnp.dot(grad_mid_b, out_weight.T, preferred_element_type=f32)
        .astype(bf16)
        .reshape(tok_rows, heads_here, HD)
    )
    delta = jnp.sum(grad_att.astype(f32) * attended.astype(f32), axis=-1)
    key_piece = lax.all_gather(keys_flat, "ctx", axis=0, tiled=True)
    value_piece = lax.all_gather(values_flat, "ctx", axis=0, tiled=True)
    seq_piece = lax.all_gather(seq_ids, "ctx", axis=0, tiled=True)
    count = key_piece.shape[0]
    key_heads = key_piece.reshape(count, heads_here, HD)
    value_heads = value_piece.reshape(count, heads_here, HD)
    gq, gk, gv = block_grads(
        query, grad_att, lse, delta, seq_ids, key_heads, value_heads, seq_piece, scale
    )
    pair = jnp.stack([gk.reshape(count, local_cols), gv.reshape(count, local_cols)], axis=1)
    own_pairs = lax.psum_scatter(
        pair.astype(jnp.bfloat16), "ctx", scatter_dimension=0, tiled=True
    ).astype(jnp.float32)
    grad_key = own_pairs[:, 0].reshape(tok_rows, heads_here, HD)
    grad_value = own_pairs[:, 1].reshape(tok_rows, heads_here, HD)
    grad_proj = jnp.stack(
        [unrotate(gq, cosine, sine), unrotate(grad_key, cosine, sine), grad_value], axis=1
    )
    grad_proj = grad_proj.astype(bf16).reshape(tok_rows, 3 * local_cols)
    grad_w_qkv = jnp.dot(first.T, grad_proj, preferred_element_type=f32).reshape(
        width, 3, local_cols
    )
    first_part = jnp.dot(grad_proj, qkv_flat.T, preferred_element_type=f32)
    attention_norm_gradient = lax.psum(first_part.astype(jnp.bfloat16), "tp").astype(jnp.float32)
    attention_normed_gradient, attention_gain_gradient = layer_normalize_backward(
        attention_norm_gradient,
        attention_standardized,
        attention_inverse_deviation,
        attention_norm_gain,
    )
    grad_tokens = grad_mid + attention_normed_gradient
    summed = (
        lax.psum(attention_gain_gradient.astype(jnp.bfloat16), "ctx").astype(jnp.float32),
        lax.psum(grad_w_qkv.astype(jnp.bfloat16), "ctx").astype(jnp.float32),
        lax.psum(grad_w_attn.astype(jnp.bfloat16), "ctx").astype(jnp.float32),
        lax.psum(feedforward_gain_gradient.astype(jnp.bfloat16), "ctx").astype(jnp.float32),
        lax.psum(grad_w_in.astype(jnp.bfloat16), "ctx").astype(jnp.float32),
        lax.psum(grad_w_out.astype(jnp.bfloat16), "ctx").astype(jnp.float32),
    )
    return (output, grad_tokens, summed[0], summed[1], summed[2], summed[3], summed[4], summed[5])


def solution(mesh):
    return jax.shard_map(
        per_device,
        mesh=mesh,
        in_specs=(
            P("ctx", None),
            P("ctx"),
            P(),
            P(None, None, "tp"),
            P("tp", None),
            P(),
            P(None, None, "tp"),
            P("tp", None),
            P("ctx", None),
        ),
        out_specs=(
            P("ctx", None),
            P("ctx", None),
            P(),
            P(None, None, "tp"),
            P("tp", None),
            P(),
            P(None, None, "tp"),
            P("tp", None),
        ),
        check_vma=False,
    )
```

profile of v0, /device:TPU:0, one launch (start us, length us, event | category | flops | bytes accessed | tf_op | source)
XLA Modules:
  0.0 697.2 jit_solution(1876158596142752087)
XLA Ops:
  7.3 4.8 copy.22
  12.6 3.0 fusion.57
  16.8 1.2 fusion.76
  18.9 1.3 slice_negate_fusion.2
  20.2 1.2 maximum_multiply_fusion.1
  22.3 1.8 slice.110
  24.1 23.5 %all-gather = s32[16,1,256]{2,1,0:T(1,128)S(1)} all-gather(s32[1,1,256]{2,1,0:T(1,128)S(1)} %bitcast.163), channel_id=1, replica_groups=mesh['ctx'=16,'tp'=2] {'ctx'}, dimensions={0}, use_global_device_ids=true | all-gather | bytes 17408 | tf_op jit(solution)/shard_map/all_gather | solution.py:119
  47.6 1.6 broadcast_compare_fusion
  49.2 28.3 %all-gather.4.cloned.1.call-done = bf16[4096,512]{0,1:T(8,128)(2,1)} async-done(((bf16[256,512]{0,1:T(8,128)(2,1)}), bf16[4096,512]{0,1:T(8,128)(2,1)}) %all-gather.4.cloned.1.call-update) | async-done | bytes 4194320 | tf_op jit(solution)/shard_map/all_gather | solution.py:117
  77.5 16.5 %select_reduce_fusion = (f32[8,256]{1,0:T(8,128)S(1)}, f32[8,256,4096]{2,1,0:T(8,128)}) fusion(pred[256,4096]{1,0:T(8,128)(4,1)} %broadcast_compare_fusion, bf16[256,8,64]{0,2,1:T(8,128)(2,1)S(1)} %get-tuple-element.38, bf16[4096,8,64]{0,2,1:T(8,128)(2,1)} %bitcast.142), kind=kOutput, calls=%fused_computation.3 | convolution fusion | flops 1098905600 | bytes 39067648 | tf_op jit(solution)/shard_map/qhd,khd->hqk/dot_general | solution.py:123
  94.6 16.2 %fusion = f32[8,256]{1,0:T(8,128)} fusion(f32[8,256,4096]{2,1,0:T(8,128)} %get-tuple-element.44, f32[8,256]{1,0:T(8,128)S(1)} %broadcast_maximum_fusion, pred[256,4096]{1,0:T(8,128)(4,1)S(1)} %copy-done.4), kind=kLoop, calls=%fused_computation.4 | loop fusion | flops 33552384 | bytes 34619392 | tf_op jit(solution)/shard_map/reduce_sum | solution.py:128
  110.8 20.1 %all-gather.6.cloned.1.call-done = bf16[4096,512]{0,1:T(8,128)(2,1)} async-done(((bf16[256,512]{0,1:T(8,128)(2,1)}), bf16[4096,512]{0,1:T(8,128)(2,1)}) %all-gather.6.cloned.1.call-update) | async-done | bytes 4194320 | tf_op jit(solution)/shard_map/all_gather | solution.py:118
  130.9 16.3 %fusion.49 = bf16[256,8,64]{0,2,1:T(8,128)(2,1)} fusion(bf16[4096,8,64]{0,2,1:T(8,128)(2,1)} %bitcast.164, f32[8,256,4096]{2,1,0:T(8,128)} %get-tuple-element.44, f32[8,256]{1,0:T(8,128)} %copy-done.29, pred[256,4096]{1,0:T(8,128)(4,1)} %broadcast_compare_fusion, f32[256,8]{0,1:T(8,128)} %bitcast.161), kind=kOutput, calls=%fused_computation.78 | convolution fusion | flops 1107558400 | bytes 39075840 | tf_op jit(solution)/shard_map/hqk,khd->hqd/dot_general | solution.py:129
  147.2 2.6 convolution_convert_fusion.4
  150.4 26.4 %all-reduce.8.cloned.1.call-done = bf16[256,1024]{1,0:T(8,128)(2,1)} async-done(((bf16[256,1024]{1,0:T(8,128)(2,1)}), bf16[256,1024]{1,0:T(8,128)(2,1)}) %all-reduce.8.cloned.1.call-update) | async-done | bytes 524304 | tf_op jit(solution)/shard_map/psum | solution.py:138
  176.8 1.3 fusion.52
  178.1 1.3 multiply_reduce_fusion
  179.5 4.5 fusion.12
  184.0 1.4 fusion.19
  186.6 5.0 fusion.27
  191.7 1.3 log_add_fusion
  193.0 27.5 %all-reduce.10.cloned.1.call-done = bf16[256,1024]{1,0:T(8,128)(2,1)} async-done(((bf16[256,1024]{1,0:T(8,128)(2,1)}), bf16[256,1024]{1,0:T(8,128)(2,1)}) %all-reduce.10.cloned.1.call-update) | async-done | bytes 524304 | tf_op jit(solution)/shard_map/psum | solution.py:165
  220.5 2.5 fusion.41
  222.9 1.8 fusion.40
  225.8 1.2 convolution_convert_fusion.7
  226.9 1.8 copy.23
  229.9 19.3 %fusion.9 = bf16[8,64,4096]{2,1,0:T(8,128)(2,1)} fusion(bf16[256,8,64]{0,2,1:T(8,128)(2,1)} %bitcast.158, f32[8,256,4096]{2,1,0:T(8,128)} %get-tuple-element.44, f32[8,256]{1,0:T(8,128)} %log_add_fusion, pred[256,4096]{1,0:T(8,128)(4,1)} %broadcast_compare_fusion), kind=kOutput, calls=%fused_computation.13 | convolution fusion | flops 1109393408 | bytes 39067648 | tf_op jit(solution)/shard_map/hqk,qhd->khd/dot_general | solution.py:74
  249.2 23.4 %multiply_convert_fusion = bf16[8,256,4096]{2,1,0:T(8,128)(2,1)} fusion(f32[8,256,4096]{2,1,0:T(8,128)} %get-tuple-element.44, f32[8,256]{1,0:T(8,128)S(1)} %bitcast.162, f32[8,256]{1,0:T(8,128)} %log_add_fusion, pred[256,4096]{1,0:T(8,128)(4,1)} %broadcast_compare_fusion, bf16[256,8,64]{0,2,1:T(8,128)(2,1)} %bitcast.159, bf16[4096,8,64]{0,2,1:T(8,128)(2,1)} %bitcast.165), kind=kOutput, calls=%fused_computation | convolution fusion | flops 1124073472 | bytes 55853056 | tf_op jit(solution)/shard_map/qhd,khd->hqk/dot_general | solution.py:77
  272.6 10.8 %multiply_convert_fusion.1 = bf16[8,64,4096]{2,1,0:T(8,128)(2,1)} fusion(bf16[256,8,64]{0,2,1:T(8,128)(2,1)S(1)} %get-tuple-element.38, bf16[8,256,4096]{2,1,0:T(8,128)(2,1)} %multiply_convert_fusion), kind=kOutput, calls=%fused_computation.12 | convolution fusion | flops 1077936128 | bytes 21233664 | tf_op jit(solution)/shard_map/hqk,qhd->khd/dot_general | solution.py:80
  283.4 7.6 %pad_maximum_fusion = bf16[4096,2,512]{0,2,1:T(8,128)(2,1)} fusion(bf16[4096,1,512]{0,2,1:T(8,128)(2,1)} %bitcast.149, bf16[4096,1,512]{0,2,1:T(8,128)(2,1)} %bitcast.144), kind=kLoop, calls=%fused_computation.11 | loop fusion | flops 4194304 | bytes 16777216 | tf_op jit(solution)/shard_map/stack | solution.py:190
  291.3 2.0 multiply_convert_fusion.2
  294.2 1.8 convolution_convert_fusion.5
  296.0 15.0 %broadcast_multiply_fusion = (f32[256,8,64]{0,2,1:T(8,128)}, f32[256,8,64]{0,2,1:T(8,128)}) fusion(f32[256,64]{0,1:T(8,128)S(1)} %copy-done.22, bf16[4096,8,64]{0,2,1:T(8,128)(2,1)} %bitcast.143, bf16[8,256,4096]{2,1,0:T(8,128)(2,1)} %multiply_convert_fusion), kind=kOutput, calls=%fused_computation.103 | convolution fusion | flops 1073872896 | bytes 22085632 | tf_op jit(solution)/shard_map/hqk,khd->qhd/dot_general | solution.py:79
  313.3 81.5 %reduce-scatter.2.cloned.1.call-done = bf16[256,2,512]{0,2,1:T(8,128)(2,1)} async-done(((bf16[4096,2,512]{0,2,1:T(8,128)(2,1)}), bf16[256,2,512]{0,2,1:T(8,128)(2,1)}) %reduce-scatter.2.cloned.1.call-update) | async-done | bytes 524304 | tf_op jit(solution)/shard_map/reduce_scatter | solution.py:191
  398.0 1.8 convolution_convert_fusion.6
  399.9 3.8 convolution_convert_fusion.1
  403.7 4.2 convolution_convert_fusion
  407.9 1.4 convolution_convert_fusion.3
  409.3 2.9 convolution_convert_fusion.2
  412.2 27.5 %all-reduce.14.cloned.1.call-done = (bf16[256,1024]{1,0:T(8,128)(2,1)}, bf16[256,1024]{1,0:T(8,128)(2,1)}) async-done(((bf16[256,1024]{1,0:T(8,128)(2,1)}, bf16[256,1024]{1,0:T(8,128)(2,1)}), (bf16[256,1024]{1,0:T(8,128)(2,1)}, bf16[256,1024]{1,0:T(8,128)(2,1)})) %all-reduce.14.cloned.1.call-update) | async-done | bytes 1048592 | tf_op jit(solution)/shard_map/psum | solution.py:152
  439.7 1.6 fusion.45
  441.3 34.7 %all-reduce = (bf16[1024]{0:T(1024)(128)(2,1)S(1)}, bf16[1024]{0:T(1024)(128)(2,1)S(1)}) all-reduce(bf16[1024]{0:T(1024)(128)(2,1)S(1)} %get-tuple-element.10, bf16[1024]{0:T(1024)(128)(2,1)S(1)} %copy-done.34), channel_id=1, replica_groups=mesh['ctx'=16,'tp'=2] {'ctx'}, use_global_device_ids=true, to_apply=%region_17.18 | all-reduce | flops 2048 | bytes 8192 | tf_op jit(solution)/shard_map/psum | solution.py:213
  477.2 3.3 fusion.44
  480.5 193.8 %all-reduce.12.cloned.1.call-done = (bf16[1024,3,512]{2,0,1:T(8,128)(2,1)}, bf16[512,1024]{1,0:T(8,128)(2,1)}, bf16[1024,2,1312]{0,2,1:T(8,128)(2,1)}, bf16[1312,1024]{1,0:T(8,128)(2,1)}) async-done(((bf16[1024,3,512]{2,0,1:T(8,128)(2,1)}, bf16[512,1024]{1,0:T(8,128)(2,1)}, bf16[1024,2,1312]{0,2,1:T(8,128)(2,1)}, bf16[1312,1024]{1,0:T(8,128)(2,1)}), (bf16[1024,3,512]{2,0,1:T(8,128)(2,1)}, ...) | async-done | bytes 12255248 | tf_op jit(solution)/shard_map/psum | solution.py:214
  674.3 5.6 convert_element_type.179
  680.0 1.6 convert_element_type.181
  681.6 5.5 convert_element_type.186
  687.1 3.1 convert_element_type.188
  (119 shorter events, 15.9 us)
Async XLA Ops:
  7.2 176.8 %copy-start = (bf16[1312,1024]{1,0:T(8,128)(2,1)S(1)}, bf16[1312,1024]{1,0:T(8,128)(2,1)}, u32[]{:S(2)}) copy-start(bf16[1312,1024]{1,0:T(8,128)(2,1)} %param.16) | copy-start | bytes 8060932
  7.2 4.9 copy-start.1
  7.2 5.4 copy-start.25
  7.2 70.3 %all-gather.4.cloned.1.call-start = ((), (), s32[]{:S(2)}) async-start(), calls=%async_computation.1 | async-start | bytes 4456448 | tf_op jit(solution)/shard_map/all_gather | solution.py:117
  12.2 3.4 copy-start.30
  12.5 3.1 copy-start.32
  15.6 1.1 copy-start.14
  18.0 6.1 copy-start.35
  18.0 3.4 copy-start.15
  18.9 2.5 copy-start.23
  22.2 108.7 %all-gather.6.cloned.1.call-start = ((), (), s32[]{:S(2)}) async-start(), calls=%async_computation.2 | async-start | bytes 4456448 | tf_op jit(solution)/shard_map/all_gather | solution.py:118
  24.1 152.8 %all-reduce.8.cloned.1.call-start = ((), (), s32[]{:S(2)}) async-start(), calls=%async_computation.3 | async-start | bytes 1048576 | tf_op jit(solution)/shard_map/psum | solution.py:138
  77.5 17.1 %copy-start.4 = (pred[256,4096]{1,0:T(8,128)(4,1)S(1)}, pred[256,4096]{1,0:T(8,128)(4,1)}, u32[]{:S(2)}) copy-start(pred[256,4096]{1,0:T(8,128)(4,1)} %broadcast_compare_fusion) | copy-start | bytes 3145732
  94.0 0.6 copy-start.29
  147.2 32.2 %copy-start.24 = (f32[1024]{0:T(1024)S(1)}, f32[1024]{0:T(1024)}, u32[]{:S(2)}) copy-start(f32[1024]{0:T(1024)} %param.14) | copy-start | bytes 12292
  149.8 70.6 %all-reduce.10.cloned.1.call-start = ((), (), s32[]{:S(2)}) async-start(), calls=%async_computation.4 | async-start | bytes 1048576 | tf_op jit(solution)/shard_map/psum | solution.py:165
  179.4 4.5 copy-start.27
  179.4 4.5 copy-start.16
  184.0 1.6 copy-start.3
  185.5 0.8 copy-start.18
  185.5 1.1 copy-start.20
  191.7 203.1 %reduce-scatter.2.cloned.1.call-start = ((), (), s32[]{:S(2)}) async-start(), calls=%async_computation.5 | async-start | bytes 8912896 | tf_op jit(solution)/shard_map/reduce_scatter | solution.py:191
  220.5 5.3 copy-start.8
  224.8 1.0 copy-start.5
  291.1 4.9 copy-start.22
  291.1 148.6 %all-reduce.14.cloned.1.call-start = ((), (), s32[]{:S(2)}) async-start(), calls=%async_computation.7 | async-start | bytes 2097152 | tf_op jit(solution)/shard_map/psum | solution.py:152
  293.4 0.8 copy-start.7
  394.8 2.2 slice-start.2
  394.8 3.2 copy-start.11
  397.1 0.9 copy-start.9
  399.8 3.9 copy-start.28
  399.8 274.5 %all-reduce.12.cloned.1.call-start = ((), (), s32[]{:S(2)}) async-start(), calls=%async_computation.6 | async-start | bytes 24510464 | tf_op jit(solution)/shard_map/psum | solution.py:214
  399.9 3.8 copy-start.2
  399.9 3.8 copy-start.19
  399.9 3.8 copy-start.21
  403.7 4.2 copy-start.6
  403.7 4.2 copy-start.13
  403.7 5.6 copy-start.10
  403.7 5.6 copy-start.26
  403.7 5.6 copy-start.31
  403.7 5.6 copy-start.33
  412.2 29.1 %copy-start.34 = (bf16[1024]{0:T(1024)(128)(2,1)S(1)}, bf16[1024]{0:T(1024)(128)(2,1)}, u32[]{:S(2)}) copy-start(bf16[1024]{0:T(1024)(128)(2,1)} %get-tuple-element.8) | copy-start | bytes 6148
  674.3 7.2 %slice-start = ((s8[5373952]{0:T(1024)(128)(4,1)}), s8[4194304]{0:T(1024)(128)(4,1)S(1)}, s32[]{:S(2)}) async-start(s8[5373952]{0:T(1024)(128)(4,1)} %bitcast.145), calls=%async_computation.8 | async-start | bytes 8388608
  674.3 5.7 copy-start.17
  674.3 7.2 %slice-start.1 = ((s8[5373952]{0:T(1024)(128)(4,1)}), s8[1179648]{0:T(1024)(128)(4,1)S(1)}, s32[]{:S(2)}) async-start(s8[5373952]{0:T(1024)(128)(4,1)} %bitcast.145), calls=%async_computation.9 | async-start | bytes 2359296
  681.6 5.5 copy-start.12
Sparse Core Ops, SparseCore 0:
  22.3 55.1 all-gather.3
  80.2 50.6 all-gather.5
  149.9 26.8 all-reduce.7
  191.8 28.6 all-reduce.9
  291.2 103.5 reduce-scatter.1
  399.9 39.7 all-reduce.13
  445.0 229.3 all-reduce.11
where the time goes:
time: 706 us; the launch traced here: 697 us
  waiting for transfers between devices  405 us (57%)
  matrix products  135 us (19%)
  other arithmetic  66.6 us (9%)
  blocking collectives  58.1 us (8%)
  local copies, waits for them, and re-layouts  16.6 us (2%)
  between operations  14.8 us (2%)
    psum x1, waiting for transfers between devices, per_device(): lax.psum(grad_w_qkv.astype(jnp.bfloat16), 'ctx').astype(jnp.float32)  194 us
    reduce_scatter x1, waiting for transfers between devices, per_device(): lax.psum_scatter(pair.astype(jnp.bfloat16), 'ctx', scatter_dimension=0, t...  81.5 us
    psum x1, blocking collectives, per_device(): lax.psum(attention_gain_gradient.astype(jnp.bfloat16), 'ctx')  34.7 us
    all_gather x1, waiting for transfers between devices, per_device(): key_piece = lax.all_gather(keys_flat, 'ctx', axis=0, tiled=True)  28.3 us
    psum x1, waiting for transfers between devices, per_device(): lax.psum(ffn_part.astype(jnp.bfloat16), 'tp').astype(jnp.float32)  27.5 us
    psum x1, waiting for transfers between devices, per_device(): lax.psum(second_part.astype(jnp.bfloat16), 'tp').astype(jnp.float32)  27.5 us
    psum x1, waiting for transfers between devices, per_device(): lax.psum(attn_part.astype(jnp.bfloat16), 'tp').astype(jnp.float32)  26.4 us
    all_gather x1, blocking collectives, per_device(): seq_piece = lax.all_gather(seq_ids, 'ctx', axis=0, tiled=True)  23.5 us
  transfers between devices with their start and end apart: 7, of which 7 were waited for; matrix products, arithmetic and copies ran while one was open for 11% of the time, Pallas kernels for 0%

commit v1 on v0

--- a/solution.py
+++ b/solution.py
@@ -211,7 +211,7 @@
     grad_tokens = grad_mid + attention_normed_gradient
     summed = (
         lax.psum(attention_gain_gradient.astype(jnp.bfloat16), "ctx").astype(jnp.float32),
-        lax.psum(grad_w_qkv.astype(jnp.bfloat16), "ctx").astype(jnp.float32),
+        jnp.sum(lax.all_gather(grad_w_qkv.astype(jnp.bfloat16), "ctx"), axis=0).astype(jnp.float32),
         lax.psum(grad_w_attn.astype(jnp.bfloat16), "ctx").astype(jnp.float32),
         lax.psum(feedforward_gain_gradient.astype(jnp.bfloat16), "ctx").astype(jnp.float32),
         lax.psum(grad_w_in.astype(jnp.bfloat16), "ctx").astype(jnp.float32),

time: 706 us -> 912 us (1.29)
  waiting for transfers between devices: 405 us -> 587 us
  other arithmetic: 66.6 us -> 89 us
    all_gather x0 -> x1, waiting for transfers between devices: none -> 209 us  [per_device(): lax.all_gather(grad_w_qkv.astype(jnp.bfloat16), 'ctx')]
    psum x1, waiting for transfers between devices: 194 us -> 175 us  [per_device(): lax.psum(grad_w_attn.astype(jnp.bfloat16), 'ctx').astype(jnp.float32)]
    reduce_sum x0 -> x1, other arithmetic: none -> 18.3 us  [per_device(): jnp.sum(lax.all_gather(grad_w_qkv.astype(jnp.bfloat16), 'ctx'), axis=0)]
    reduce_scatter x1, waiting for transfers between devices: 81.5 us -> 71.2 us  [per_device(): lax.psum_scatter(pair.astype(jnp.bfloat16), 'ctx', scatter_dimension=0, t...]
  transfers between devices with their start and end apart: 7 -> 8, of which waited for: 7 -> 8; matrix products, arithmetic and copies ran while one was open for 11% -> 11% of each run, Pallas kernels for 0% -> 0%
where the time goes in v1:
time: 912 us; the launch traced here: 903 us
  waiting for transfers between devices  587 us (64%)
  matrix products  136 us (15%)
  other arithmetic  89 us (10%)
  blocking collectives  57.9 us (6%)
  local copies, waits for them, and re-layouts  16.5 us (2%)
  between operations  15 us (2%)
    all_gather x1, waiting for transfers between devices, per_device(): lax.all_gather(grad_w_qkv.astype(jnp.bfloat16), 'ctx')  209 us
    psum x1, waiting for transfers between devices, per_device(): lax.psum(grad_w_attn.astype(jnp.bfloat16), 'ctx').astype(jnp.float32)  175 us
    reduce_scatter x1, waiting for transfers between devices, per_device(): lax.psum_scatter(pair.astype(jnp.bfloat16), 'ctx', scatter_dimension=0, t...  71.2 us
    psum x1, blocking collectives, per_device(): lax.psum(attention_gain_gradient.astype(jnp.bfloat16), 'ctx')  34.4 us
    psum x1, waiting for transfers between devices, per_device(): lax.psum(ffn_part.astype(jnp.bfloat16), 'tp').astype(jnp.float32)  29 us
    all_gather x1, waiting for transfers between devices, per_device(): key_piece = lax.all_gather(keys_flat, 'ctx', axis=0, tiled=True)  28.3 us
    psum x1, waiting for transfers between devices, per_device(): lax.psum(second_part.astype(jnp.bfloat16), 'tp').astype(jnp.float32)  27.5 us
    psum x1, waiting for transfers between devices, per_device(): lax.psum(attn_part.astype(jnp.bfloat16), 'tp').astype(jnp.float32)  26.4 us
  transfers between devices with their start and end apart: 8, of which 8 were waited for; matrix products, arithmetic and copies ran while one was open for 11% of the time, Pallas kernels for 0%

profile of v1, /device:TPU:0, one launch (start us, length us, event | category | flops | bytes accessed | tf_op | source)
XLA Modules:
  0.0 902.6 jit_solution(1810867299860743567)
XLA Ops:
  7.3 4.8 copy.22
  12.5 3.0 fusion.57
  18.9 1.3 slice_negate_fusion.2
  22.2 1.8 slice.110
  24.1 23.5 %all-gather.1 = s32[16,1,256]{2,1,0:T(1,128)S(1)} all-gather(s32[1,1,256]{2,1,0:T(1,128)S(1)} %bitcast.163), channel_id=1, replica_groups=mesh['ctx'=16,'tp'=2] {'ctx'}, dimensions={0}, use_global_device_ids=true | all-gather | bytes 17408 | tf_op jit(solution)/shard_map/all_gather | solution.py:119
  47.5 1.6 broadcast_compare_fusion
  49.2 28.3 %all-gather.6.cloned.1.call-done = bf16[4096,512]{0,1:T(8,128)(2,1)} async-done(((bf16[256,512]{0,1:T(8,128)(2,1)}), bf16[4096,512]{0,1:T(8,128)(2,1)}) %all-gather.6.cloned.1.call-update) | async-done | bytes 4194320 | tf_op jit(solution)/shard_map/all_gather | solution.py:117
  77.5 16.5 %select_reduce_fusion = (f32[8,256]{1,0:T(8,128)S(1)}, f32[8,256,4096]{2,1,0:T(8,128)}) fusion(pred[256,4096]{1,0:T(8,128)(4,1)} %broadcast_compare_fusion, bf16[256,8,64]{0,2,1:T(8,128)(2,1)S(1)} %get-tuple-element.37, bf16[4096,8,64]{0,2,1:T(8,128)(2,1)} %bitcast.144), kind=kOutput, calls=%fused_computation.3 | convolution fusion | flops 1098905600 | bytes 39067648 | tf_op jit(solution)/shard_map/qhd,khd->hqk/dot_general | solution.py:123
  94.6 16.2 %fusion = f32[8,256]{1,0:T(8,128)} fusion(f32[8,256,4096]{2,1,0:T(8,128)} %get-tuple-element.43, f32[8,256]{1,0:T(8,128)S(1)} %broadcast_maximum_fusion, pred[256,4096]{1,0:T(8,128)(4,1)S(1)} %copy-done.4), kind=kLoop, calls=%fused_computation.4 | loop fusion | flops 33552384 | bytes 34619392 | tf_op jit(solution)/shard_map/reduce_sum | solution.py:128
  110.8 20.1 %all-gather.8.cloned.1.call-done = bf16[4096,512]{0,1:T(8,128)(2,1)} async-done(((bf16[256,512]{0,1:T(8,128)(2,1)}), bf16[4096,512]{0,1:T(8,128)(2,1)}) %all-gather.8.cloned.1.call-update) | async-done | bytes 4194320 | tf_op jit(solution)/shard_map/all_gather | solution.py:118
  130.9 16.2 %fusion.49 = bf16[256,8,64]{0,2,1:T(8,128)(2,1)} fusion(bf16[4096,8,64]{0,2,1:T(8,128)(2,1)} %bitcast.164, f32[8,256,4096]{2,1,0:T(8,128)} %get-tuple-element.43, f32[8,256]{1,0:T(8,128)} %copy-done.27, pred[256,4096]{1,0:T(8,128)(4,1)} %broadcast_compare_fusion, f32[256,8]{0,1:T(8,128)} %bitcast.161), kind=kOutput, calls=%fused_computation.78 | convolution fusion | flops 1107558400 | bytes 39075840 | tf_op jit(solution)/shard_map/hqk,khd->hqd/dot_general | solution.py:129
  147.0 2.6 convolution_convert_fusion.4
  150.2 26.4 %all-reduce.8.cloned.1.call-done = bf16[256,1024]{1,0:T(8,128)(2,1)} async-done(((bf16[256,1024]{1,0:T(8,128)(2,1)}), bf16[256,1024]{1,0:T(8,128)(2,1)}) %all-reduce.8.cloned.1.call-update) | async-done | bytes 524304 | tf_op jit(solution)/shard_map/psum | solution.py:138
  176.6 1.3 fusion.52
  177.9 1.3 multiply_reduce_fusion
  179.3 4.5 fusion.12
  183.8 1.4 fusion.19
  186.4 5.0 fusion.27
  191.5 1.3 log_add_fusion
  192.8 27.5 %all-reduce.10.cloned.1.call-done = bf16[256,1024]{1,0:T(8,128)(2,1)} async-done(((bf16[256,1024]{1,0:T(8,128)(2,1)}), bf16[256,1024]{1,0:T(8,128)(2,1)}) %all-reduce.10.cloned.1.call-update) | async-done | bytes 524304 | tf_op jit(solution)/shard_map/psum | solution.py:165
  220.2 2.5 fusion.41
  222.7 1.8 fusion.40
  226.7 1.8 copy.23
  229.6 19.0 %fusion.9 = bf16[8,64,4096]{2,1,0:T(8,128)(2,1)} fusion(bf16[256,8,64]{0,2,1:T(8,128)(2,1)} %bitcast.158, f32[8,256,4096]{2,1,0:T(8,128)} %get-tuple-element.43, f32[8,256]{1,0:T(8,128)} %log_add_fusion, pred[256,4096]{1,0:T(8,128)(4,1)} %broadcast_compare_fusion), kind=kOutput, calls=%fused_computation.13 | convolution fusion | flops 1109393408 | bytes 39067648 | tf_op jit(solution)/shard_map/hqk,qhd->khd/dot_general | solution.py:74
  248.7 23.4 %multiply_convert_fusion = bf16[8,256,4096]{2,1,0:T(8,128)(2,1)} fusion(f32[8,256,4096]{2,1,0:T(8,128)} %get-tuple-element.43, f32[8,256]{1,0:T(8,128)S(1)} %bitcast.162, f32[8,256]{1,0:T(8,128)} %log_add_fusion, pred[256,4096]{1,0:T(8,128)(4,1)} %broadcast_compare_fusion, bf16[256,8,64]{0,2,1:T(8,128)(2,1)} %bitcast.159, bf16[4096,8,64]{0,2,1:T(8,128)(2,1)} %bitcast.165), kind=kOutput, calls=%fused_computation | convolution fusion | flops 1124073472 | bytes 55853056 | tf_op jit(solution)/shard_map/qhd,khd->hqk/dot_general | solution.py:77
  272.1 10.8 %multiply_convert_fusion.1 = bf16[8,64,4096]{2,1,0:T(8,128)(2,1)} fusion(bf16[256,8,64]{0,2,1:T(8,128)(2,1)S(1)} %get-tuple-element.37, bf16[8,256,4096]{2,1,0:T(8,128)(2,1)} %multiply_convert_fusion), kind=kOutput, calls=%fused_computation.12 | convolution fusion | flops 1077936128 | bytes 21233664 | tf_op jit(solution)/shard_map/hqk,qhd->khd/dot_general | solution.py:80
  282.9 7.6 pad_maximum_fusion
  290.8 2.0 multiply_convert_fusion.2
  293.7 3.6 convolution_convert_fusion.1
  297.3 4.2 convolution_convert_fusion
  301.5 1.4 convolution_convert_fusion.3
  303.0 2.9 convolution_convert_fusion.5
  305.9 14.8 %broadcast_multiply_fusion = (f32[256,8,64]{0,2,1:T(8,128)}, f32[256,8,64]{0,2,1:T(8,128)}) fusion(f32[256,64]{0,1:T(8,128)S(1)} %copy-done.20, bf16[4096,8,64]{0,2,1:T(8,128)(2,1)} %bitcast.145, bf16[8,256,4096]{2,1,0:T(8,128)(2,1)} %multiply_convert_fusion), kind=kOutput, calls=%fused_computation.103 | convolution fusion | flops 1073872896 | bytes 22085632 | tf_op jit(solution)/shard_map/hqk,khd->qhd/dot_general | solution.py:79
  321.8 1.3 fusion.56
  323.1 71.2 %reduce-scatter.2.cloned.1.call-done = bf16[256,2,512]{0,2,1:T(8,128)(2,1)} async-done(((bf16[4096,2,512]{0,2,1:T(8,128)(2,1)}), bf16[256,2,512]{0,2,1:T(8,128)(2,1)}) %reduce-scatter.2.cloned.1.call-update) | async-done | bytes 524304 | tf_op jit(solution)/shard_map/reduce_scatter | solution.py:191
  397.5 1.8 convolution_convert_fusion.6
  399.7 4.0 convolution_convert_fusion.2
  403.7 175.3 %all-reduce.12.cloned.1.call-done = (bf16[512,1024]{1,0:T(8,128)(2,1)}, bf16[1024,2,1312]{0,2,1:T(8,128)(2,1)}, bf16[1312,1024]{1,0:T(8,128)(2,1)}) async-done(((bf16[512,1024]{1,0:T(8,128)(2,1)}, bf16[1024,2,1312]{0,2,1:T(8,128)(2,1)}, bf16[1312,1024]{1,0:T(8,128)(2,1)}), (bf16[512,1024]{1,0:T(8,128)(2,1)}, bf16[1024,2,1312]{0,2,1:T(8,128)(2,1)}, ...) | async-done | bytes 9109520 | tf_op jit(solution)/shard_map/psum | solution.py:215
  579.0 2.8 convert_element_type.183
  581.8 8.2 convert_element_type.188
  590.0 3.1 convert_element_type.190
  593.1 29.0 %all-reduce.14.cloned.1.call-done = (bf16[256,1024]{1,0:T(8,128)(2,1)}, bf16[256,1024]{1,0:T(8,128)(2,1)}) async-done(((bf16[256,1024]{1,0:T(8,128)(2,1)}, bf16[256,1024]{1,0:T(8,128)(2,1)}), (bf16[256,1024]{1,0:T(8,128)(2,1)}, bf16[256,1024]{1,0:T(8,128)(2,1)})) %all-reduce.14.cloned.1.call-update) | async-done | bytes 1048592 | tf_op jit(solution)/shard_map/psum | solution.py:152
  622.1 1.6 fusion.45
  623.7 34.4 %all-reduce = (bf16[1024]{0:T(1024)(128)(2,1)S(1)}, bf16[1024]{0:T(1024)(128)(2,1)S(1)}) all-reduce(bf16[1024]{0:T(1024)(128)(2,1)S(1)} %get-tuple-element.10, bf16[1024]{0:T(1024)(128)(2,1)S(1)} %copy-done.32), channel_id=1, replica_groups=mesh['ctx'=16,'tp'=2] {'ctx'}, use_global_device_ids=true, to_apply=%region_17.18 | all-reduce | flops 2048 | bytes 8192 | tf_op jit(solution)/shard_map/psum | solution.py:213
  659.3 3.5 fusion.44
  662.8 208.7 %all-gather.10.cloned.1.call-done = bf16[16384,3,512]{2,0,1:T(8,128)(2,1)} async-done(((bf16[1024,3,512]{2,0,1:T(8,128)(2,1)}), bf16[16384,3,512]{2,0,1:T(8,128)(2,1)}) %all-gather.10.cloned.1.call-update) | async-done | bytes 50331664 | tf_op jit(solution)/shard_map/all_gather | solution.py:214
  871.5 18.3 %reduce_sum.131 = bf16[1024,3,512]{2,0,1:T(8,128)(2,1)} reduce(bf16[16,1024,3,512]{3,1,0,2:T(8,128)(2,1)} %bitcast.143, bf16[]{:T(256)} %constant.46.clone.1), dimensions={0}, to_apply=%region_18.19 | reduce | flops 23592960 | bytes 53477376 | tf_op jit(solution)/shard_map/reduce_sum | solution.py:214
  889.8 5.5 convert_element_type.181
  (114 shorter events, 18.5 us)
Async XLA Ops:
  7.2 176.6 %copy-start = (bf16[1312,1024]{1,0:T(8,128)(2,1)S(1)}, bf16[1312,1024]{1,0:T(8,128)(2,1)}, u32[]{:S(2)}) copy-start(bf16[1312,1024]{1,0:T(8,128)(2,1)} %param.16) | copy-start | bytes 8060932
  7.2 4.9 copy-start.1
  7.2 5.3 copy-start.23
  7.2 70.3 %all-gather.6.cloned.1.call-start = ((), (), s32[]{:S(2)}) async-start(), calls=%async_computation.1 | async-start | bytes 4456448 | tf_op jit(solution)/shard_map/all_gather | solution.py:117
  12.2 3.4 copy-start.28
  12.5 3.1 copy-start.30
  15.6 1.1 copy-start.13
  18.0 6.1 copy-start.33
  18.0 3.4 copy-start.14
  18.9 2.5 copy-start.21
  22.2 108.7 %all-gather.8.cloned.1.call-start = ((), (), s32[]{:S(2)}) async-start(), calls=%async_computation.2 | async-start | bytes 4456448 | tf_op jit(solution)/shard_map/all_gather | solution.py:118
  24.0 152.6 %all-reduce.8.cloned.1.call-start = ((), (), s32[]{:S(2)}) async-start(), calls=%async_computation.3 | async-start | bytes 1048576 | tf_op jit(solution)/shard_map/psum | solution.py:138
  77.5 17.1 %copy-start.4 = (pred[256,4096]{1,0:T(8,128)(4,1)S(1)}, pred[256,4096]{1,0:T(8,128)(4,1)}, u32[]{:S(2)}) copy-start(pred[256,4096]{1,0:T(8,128)(4,1)} %broadcast_compare_fusion) | copy-start | bytes 3145732
  94.0 0.6 copy-start.27
  147.0 32.2 %copy-start.22 = (f32[1024]{0:T(1024)S(1)}, f32[1024]{0:T(1024)}, u32[]{:S(2)}) copy-start(f32[1024]{0:T(1024)} %param.14) | copy-start | bytes 12292
  149.6 70.6 %all-reduce.10.cloned.1.call-start = ((), (), s32[]{:S(2)}) async-start(), calls=%async_computation.4 | async-start | bytes 1048576 | tf_op jit(solution)/shard_map/psum | solution.py:165
  179.2 4.5 copy-start.25
  179.3 4.5 copy-start.15
  183.8 1.5 copy-start.3
  185.3 0.8 copy-start.16
  185.3 1.1 copy-start.18
  191.4 202.9 %reduce-scatter.2.cloned.1.call-start = ((), (), s32[]{:S(2)}) async-start(), calls=%async_computation.5 | async-start | bytes 8912896 | tf_op jit(solution)/shard_map/reduce_scatter | solution.py:191
  220.2 5.3 copy-start.8
  224.5 1.0 copy-start.5
  290.6 288.5 %all-reduce.12.cloned.1.call-start = ((), (), s32[]{:S(2)}) async-start(), calls=%async_computation.7 | async-start | bytes 18219008 | tf_op jit(solution)/shard_map/psum | solution.py:215
  292.8 0.8 copy-start.7
  293.7 3.6 copy-start.2
  293.7 3.6 copy-start.17
  293.7 3.6 copy-start.19
  293.7 3.6 copy-start.26
  297.3 4.2 copy-start.6
  297.3 4.2 copy-start.12
  302.9 3.0 copy-start.20
  302.9 319.2 %all-reduce.14.cloned.1.call-start = ((), (), s32[]{:S(2)}) async-start(), calls=%async_computation.8 | async-start | bytes 2097152 | tf_op jit(solution)/shard_map/psum | solution.py:152
  394.3 2.2 slice-start
  394.3 3.2 copy-start.10
  396.5 3.2 copy-start.24
  396.5 3.1 copy-start.29
  396.5 3.1 copy-start.31
  396.6 0.9 copy-start.9
  399.3 472.2 %all-gather.10.cloned.1.call-start = ((), (), s32[]{:S(2)}) async-start(), calls=%async_computation.6 | async-start | bytes 53477376 | tf_op jit(solution)/shard_map/all_gather | solution.py:214
  581.8 8.2 copy-start.11
  590.0 33.6 %copy-start.32 = (bf16[1024]{0:T(1024)(128)(2,1)S(1)}, bf16[1024]{0:T(1024)(128)(2,1)}, u32[]{:S(2)}) copy-start(bf16[1024]{0:T(1024)(128)(2,1)} %get-tuple-element.8) | copy-start | bytes 6148
Sparse Core Ops, SparseCore 0:
  22.3 55.1 all-gather.5
  80.2 50.6 all-gather.7
  149.8 26.8 all-reduce.7
  191.5 28.6 all-reduce.9
  290.7 103.6 reduce-scatter.1
  398.8 180.1 all-reduce.11
  582.0 40.0 all-reduce.13
  624.2 247.2 all-gather.9
